TPU v7x, 32 devices: a whole 2x2x4 slice. The times are simulated.
32 devices in a mesh: gy: 8 (over y, x, core), gx: 4 (over z).
Axes of the slice: x: 2, y: 2, z: 4, core: 2. Of those that a mesh axis runs over, the one named last changes fastest.
Arguments:
- level_set: float32 [128, 8192], P('gy', 'gx'), may hold values from -6 to 6
- spread_rate: float32 [128, 8192], P('gy', 'gx'), may hold values from 0.2 to 2
- cotangent: float32 [128, 8192], P('gy', 'gx'), may hold values from -6 to 6
Outputs:
- final_state: float32 [128, 8192], P('gy', 'gx')
- rate_gradient: float32 [128, 8192], P('gy', 'gx')
- initial_gradient: float32 [128, 8192], P('gy', 'gx')
All inputs are finite; a program needn't handle non-finite values.
Results may differ from a plain program's by a relative error of at most 0.000029.
Values sent between devices are 32-bit elements; how exact they have to be, the bound alone decides.
A program may use at most 128 MiB of HBM per device.

v0:
```python
import jax
import jax.numpy as jnp
from jax import lax
from jax.sharding import PartitionSpec as P

STEPS = 6


time_step = 0.2
smooth_eps = 0.001
speed_floor = 0.25


def extended(block, sides, width):
    for axis, dim in sides:
        count = lax.axis_size(axis)
        forward = [(i, i + 1) for i in range(count - 1)]
        forward.append((count - 1, 0))
        backward = [(target, source) for source, target in forward]
        low = lax.ppermute(
            lax.slice_in_dim(block, block.shape[dim] - width, None, axis=dim), axis, forward
        )
        high = lax.ppermute(lax.slice_in_dim(block, 0, width, axis=dim), axis, backward)
        block = jnp.concatenate([low, block, high], axis=dim)
    return block


def weno(first, second, third, fourth, fifth):
    cand_one = first / 3.0 - 7.0 * second / 6.0 + 11.0 * third / 6.0
    cand_two = -second / 6.0 + 5.0 * third / 6.0 + fourth / 3.0
    cand_three = third / 3.0 + 5.0 * fourth / 6.0 - fifth / 6.0
    beta_one = (
        13.0 / 12.0 * (first - 2.0 * second + third) ** 2
        + 0.25 * (first - 4.0 * second + 3.0 * third) ** 2
    )
    beta_two = 13.0 / 12.0 * (second - 2.0 * third + fourth) ** 2 + 0.25 * (second - fourth) ** 2
    beta_three = (
        13.0 / 12.0 * (third - 2.0 * fourth + fifth) ** 2
        + 0.25 * (3.0 * third - 4.0 * fourth + fifth) ** 2
    )
    alpha_one = 0.1 / (smooth_eps + beta_one) ** 2
    alpha_two = 0.6 / (smooth_eps + beta_two) ** 2
    alpha_three = 0.3 / (smooth_eps + beta_three) ** 2
    return (alpha_one * cand_one + alpha_two * cand_two + alpha_three * cand_three) / (
        alpha_one + alpha_two + alpha_three
    )


def sides_rows(diffs, count):
    left = weno(
        diffs[0:count],
        diffs[1 : count + 1],
        diffs[2 : count + 2],
        diffs[3 : count + 3],
        diffs[4 : count + 4],
    )
    right = weno(
        diffs[5 : count + 5],
        diffs[4 : count + 4],
        diffs[3 : count + 3],
        diffs[2 : count + 2],
        diffs[1 : count + 1],
    )
    return (left, right)


def sides_cols(diffs, count):
    left = weno(
        diffs[:, 0:count],
        diffs[:, 1 : count + 1],
        diffs[:, 2 : count + 2],
        diffs[:, 3 : count + 3],
        diffs[:, 4 : count + 4],
    )
    right = weno(
        diffs[:, 5 : count + 5],
        diffs[:, 4 : count + 4],
        diffs[:, 3 : count + 3],
        diffs[:, 2 : count + 2],
        diffs[:, 1 : count + 1],
    )
    return (left, right)


def speed(padded):
    row_count = padded.shape[0] - 6
    col_count = padded.shape[1] - 6
    column_band = padded[:, 3 : 3 + col_count]
    left_y, right_y = sides_rows(column_band[1:] - column_band[:-1], row_count)
    row_band = padded[3 : 3 + row_count, :]
    left_x, right_x = sides_cols(row_band[:, 1:] - row_band[:, :-1], col_count)
    square = jnp.maximum(left_y, 0.0) ** 2 + jnp.minimum(right_y, 0.0) ** 2
    square = square + jnp.maximum(left_x, 0.0) ** 2 + jnp.minimum(right_x, 0.0) ** 2
    return jnp.sqrt(square + speed_floor)


def faces(state):
    deep = extended(state, (("gy", 0), ("gx", 1)), 6)
    return (deep[3:-3, 3:-3], deep)


def adjoint_reuse(deep, weighted):
    weighted_pad = extended(weighted, (("gy", 0), ("gx", 1)), 3)
    cycle, pull_back = jax.vjp(speed, deep)
    (grad_deep,) = pull_back(weighted_pad)
    return (grad_deep[6:-6, 6:-6], cycle[3:-3, 3:-3])


def shards(level_set, spread_rate, cotangent):
    stored = []
    state = level_set
    for step in range(STEPS):
        padded, kept = faces(state)
        stored.append((state, kept))
        middle = state - time_step * spread_rate * speed(padded)
        padded_mid, kept_mid = faces(middle)
        stored.append((middle, kept_mid))
        state = 0.5 * state + 0.5 * (middle - time_step * spread_rate * speed(padded_mid))

    def adjoint(entry, weight):
        return adjoint_reuse(entry[1], spread_rate * weight)

    adjoint_state = cotangent
    rate_gradient = jnp.zeros_like(spread_rate)
    for step in reversed(range(STEPS)):
        weight_late = 0.5 * time_step * adjoint_state
        back_late, value_late = adjoint(stored[2 * step + 1], weight_late)
        adjoint_middle = 0.5 * adjoint_state - back_late
        rate_gradient = rate_gradient - weight_late * value_late
        weight_early = time_step * adjoint_middle
        back_early, value_early = adjoint(stored[2 * step], weight_early)
        rate_gradient = rate_gradient - weight_early * value_early
        adjoint_state = 0.5 * adjoint_state + adjoint_middle - back_early
    return (state, rate_gradient, adjoint_state)


def solution(mesh):
    in_specs = (P("gy", "gx"), P("gy", "gx"), P("gy", "gx"))
    out_specs = (P("gy", "gx"), P("gy", "gx"), P("gy", "gx"))
    return jax.shard_map(shards, mesh=mesh, in_specs=in_specs, out_specs=out_specs, check_vma=False)
```

profile of v0, /device:TPU:0, one launch (start us, length us, event | category | flops | bytes accessed | tf_op | source)
XLA Modules:
  0.0 438.0 jit_solution(8697508681811381060)
XLA Ops:
  2.1 2.9 collective-permute-start.1
  37.0 2.9 collective-permute-start.51
  40.1 3.8 collective-permute-start.11
  52.0 3.9 collective-permute-start.15
  65.4 3.2 collective-permute-start.19
  77.6 3.0 collective-permute-start.23
  90.1 3.0 collective-permute-start.27
  102.1 3.0 collective-permute-start.31
  114.5 3.0 collective-permute-start.35
  126.5 13.5 %collective-permute-start.39 = (f32[28,6]{1,0:T(8,128)S(1)}, f32[28,6]{1,0:T(8,128)S(1)}, u32[]{:S(2)}, u32[]{:S(2)}) collective-permute-start(f32[28,6]{1,0:T(8,128)S(1)} %get-tuple-element.1103), channel_id=1, source_target_pairs={{1,0},{2,1},{3,2},{0,3},{5,4},{6,5},{7,6},{4,7},{9,8},{10,9},{11,1... | collective-permute-start | bytes 2024 | tf_op jit(solution)/shard_map/ppermute | solution.py:23
  150.7 3.1 collective-permute-start.43
  164.8 3.0 collective-permute-start.47
  188.7 3.5 collective-permute-start.55
  195.4 4.4 multiply_add_fusion.299
  213.8 4.3 collective-permute-start.59
  221.2 4.1 multiply_add_fusion.271
  239.3 4.0 collective-permute-start.63
  246.4 4.0 multiply_add_fusion.243
  264.3 4.1 collective-permute-start.67
  271.4 3.8 multiply_add_fusion.215
  288.4 4.3 collective-permute-start.71
  295.8 3.8 multiply_add_fusion.187
  311.8 3.5 collective-permute-start.75
  316.9 3.7 multiply_add_fusion.159
  332.7 3.0 collective-permute-start.79
  337.3 3.7 multiply_add_fusion.131
  353.3 3.1 collective-permute-start.83
  358.6 3.8 multiply_add_fusion.103
  380.4 3.8 multiply_add_fusion.75
  397.3 2.9 collective-permute-start.91
  420.3 2.9 collective-permute-start.95
  425.5 3.1 multiply_add_fusion.19
  (736 shorter events, 312.9 us)
Async XLA Ops:
  7.1 6.3 %collective-permute-start.2 = (f32[28,6]{1,0:T(8,128)S(1)}, f32[28,6]{1,0:T(8,128)S(1)}, u32[]{:S(2)}, u32[]{:S(2)}) collective-permute-start(f32[28,6]{1,0:T(8,128)S(1)} %get-tuple-element.1122), channel_id=1, source_target_pairs={{0,1},{1,2},{2,3},{3,0},{4,5},{5,6},{6,7},{7,4},{8,9},{9,10},{10,1... | collective-permute-start | bytes 2024 | tf_op jit(solution)/shard_map/ppermute | solution.py:20
  20.7 5.6 %collective-permute-start.6 = (f32[28,6]{1,0:T(8,128)S(1)}, f32[28,6]{1,0:T(8,128)S(1)}, u32[]{:S(2)}, u32[]{:S(2)}) collective-permute-start(f32[28,6]{1,0:T(8,128)S(1)} %get-tuple-element.1120), channel_id=1, source_target_pairs={{0,1},{1,2},{2,3},{3,0},{4,5},{5,6},{6,7},{7,4},{8,9},{9,10},{10,1... | collective-permute-start | bytes 2024 | tf_op jit(solution)/shard_map/ppermute | solution.py:20
  28.9 7.1 %collective-permute-start.48 = (f32[3,2048]{1,0:T(4,128)S(1)}, f32[3,2048]{1,0:T(4,128)S(1)}, u32[]{:S(2)}, u32[]{:S(2)}) collective-permute-start(f32[3,2048]{1,0:T(4,128)S(1)} %get-tuple-element.1218), channel_id=1, source_target_pairs={{0,4},{4,8},{8,12},{12,16},{16,20},{20,24},{24,28},{28,0},{1,5},{5... | collective-permute-start | bytes 73736 | tf_op jit(solution)/shard_map/ppermute | solution.py:20
  29.0 7.0 %collective-permute-start.49 = (f32[3,2048]{1,0:T(4,128)S(1)}, f32[3,2048]{1,0:T(4,128)S(1)}, u32[]{:S(2)}, u32[]{:S(2)}) collective-permute-start(f32[3,2048]{1,0:T(4,128)S(1)} %get-tuple-element.1219), channel_id=1, source_target_pairs={{4,0},{8,4},{12,8},{16,12},{20,16},{24,20},{28,24},{0,28},{5,1},{9... | collective-permute-start | bytes 73736 | tf_op jit(solution)/shard_map/ppermute | solution.py:23
  31.6 8.3 %collective-permute-start.8 = (f32[6,2048]{1,0:T(8,128)S(1)}, f32[6,2048]{1,0:T(8,128)S(1)}, u32[]{:S(2)}, u32[]{:S(2)}) collective-permute-start(f32[6,2048]{1,0:T(8,128)S(1)} %get-tuple-element.1239), channel_id=1, source_target_pairs={{0,4},{4,8},{8,12},{12,16},{16,20},{20,24},{24,28},{28,0},{1,5},{5... | collective-permute-start | bytes 147464 | tf_op jit(solution)/shard_map/ppermute | solution.py:20
  31.7 8.2 %collective-permute-start.9 = (f32[6,2048]{1,0:T(8,128)S(1)}, f32[6,2048]{1,0:T(8,128)S(1)}, u32[]{:S(2)}, u32[]{:S(2)}) collective-permute-start(f32[6,2048]{1,0:T(8,128)S(1)} %get-tuple-element.1240), channel_id=1, source_target_pairs={{4,0},{8,4},{12,8},{16,12},{20,16},{24,20},{28,24},{0,28},{5,1},{9... | collective-permute-start | bytes 147464 | tf_op jit(solution)/shard_map/ppermute | solution.py:23
  36.1 14.8 %collective-permute-start.50 = (f32[22,3]{1,0:T(8,128)S(1)}, f32[22,3]{1,0:T(8,128)S(1)}, u32[]{:S(2)}, u32[]{:S(2)}) collective-permute-start(f32[22,3]{1,0:T(8,128)S(1)} %get-tuple-element.1194), channel_id=1, source_target_pairs={{0,1},{1,2},{2,3},{3,0},{4,5},{5,6},{6,7},{7,4},{8,9},{9,10},{10,1... | collective-permute-start | bytes 800 | tf_op jit(solution)/shard_map/ppermute | solution.py:20
  37.0 13.8 %collective-permute-start.51 = (f32[22,3]{1,0:T(8,128)S(1)}, f32[22,3]{1,0:T(8,128)S(1)}, u32[]{:S(2)}, u32[]{:S(2)}) collective-permute-start(f32[22,3]{1,0:T(8,128)S(1)} %get-tuple-element.1193), channel_id=1, source_target_pairs={{1,0},{2,1},{3,2},{0,3},{5,4},{6,5},{7,6},{4,7},{9,8},{10,9},{11,1... | collective-permute-start | bytes 800 | tf_op jit(solution)/shard_map/ppermute | solution.py:23
  40.1 5.5 %collective-permute-start.10 = (f32[28,6]{1,0:T(8,128)S(1)}, f32[28,6]{1,0:T(8,128)S(1)}, u32[]{:S(2)}, u32[]{:S(2)}) collective-permute-start(f32[28,6]{1,0:T(8,128)S(1)} %get-tuple-element.1118), channel_id=1, source_target_pairs={{0,1},{1,2},{2,3},{3,0},{4,5},{5,6},{6,7},{7,4},{8,9},{9,10},{10,1... | collective-permute-start | bytes 2024 | tf_op jit(solution)/shard_map/ppermute | solution.py:20
  40.1 5.5 %collective-permute-start.11 = (f32[28,6]{1,0:T(8,128)S(1)}, f32[28,6]{1,0:T(8,128)S(1)}, u32[]{:S(2)}, u32[]{:S(2)}) collective-permute-start(f32[28,6]{1,0:T(8,128)S(1)} %get-tuple-element.1117), channel_id=1, source_target_pairs={{1,0},{2,1},{3,2},{0,3},{5,4},{6,5},{7,6},{4,7},{9,8},{10,9},{11,1... | collective-permute-start | bytes 2024 | tf_op jit(solution)/shard_map/ppermute | solution.py:23
  52.0 5.5 %collective-permute-start.14 = (f32[28,6]{1,0:T(8,128)S(1)}, f32[28,6]{1,0:T(8,128)S(1)}, u32[]{:S(2)}, u32[]{:S(2)}) collective-permute-start(f32[28,6]{1,0:T(8,128)S(1)} %get-tuple-element.1116), channel_id=1, source_target_pairs={{0,1},{1,2},{2,3},{3,0},{4,5},{5,6},{6,7},{7,4},{8,9},{9,10},{10,1... | collective-permute-start | bytes 2024 | tf_op jit(solution)/shard_map/ppermute | solution.py:20
  64.5 5.5 %collective-permute-start.18 = (f32[28,6]{1,0:T(8,128)S(1)}, f32[28,6]{1,0:T(8,128)S(1)}, u32[]{:S(2)}, u32[]{:S(2)}) collective-permute-start(f32[28,6]{1,0:T(8,128)S(1)} %get-tuple-element.1114), channel_id=1, source_target_pairs={{0,1},{1,2},{2,3},{3,0},{4,5},{5,6},{6,7},{7,4},{8,9},{9,10},{10,1... | collective-permute-start | bytes 2024 | tf_op jit(solution)/shard_map/ppermute | solution.py:20
  76.6 5.7 %collective-permute-start.22 = (f32[28,6]{1,0:T(8,128)S(1)}, f32[28,6]{1,0:T(8,128)S(1)}, u32[]{:S(2)}, u32[]{:S(2)}) collective-permute-start(f32[28,6]{1,0:T(8,128)S(1)} %get-tuple-element.1112), channel_id=1, source_target_pairs={{0,1},{1,2},{2,3},{3,0},{4,5},{5,6},{6,7},{7,4},{8,9},{9,10},{10,1... | collective-permute-start | bytes 2024 | tf_op jit(solution)/shard_map/ppermute | solution.py:20
  89.2 5.5 %collective-permute-start.26 = (f32[28,6]{1,0:T(8,128)S(1)}, f32[28,6]{1,0:T(8,128)S(1)}, u32[]{:S(2)}, u32[]{:S(2)}) collective-permute-start(f32[28,6]{1,0:T(8,128)S(1)} %get-tuple-element.1110), channel_id=1, source_target_pairs={{0,1},{1,2},{2,3},{3,0},{4,5},{5,6},{6,7},{7,4},{8,9},{9,10},{10,1... | collective-permute-start | bytes 2024 | tf_op jit(solution)/shard_map/ppermute | solution.py:20
  101.2 5.5 %collective-permute-start.30 = (f32[28,6]{1,0:T(8,128)S(1)}, f32[28,6]{1,0:T(8,128)S(1)}, u32[]{:S(2)}, u32[]{:S(2)}) collective-permute-start(f32[28,6]{1,0:T(8,128)S(1)} %get-tuple-element.1108), channel_id=1, source_target_pairs={{0,1},{1,2},{2,3},{3,0},{4,5},{5,6},{6,7},{7,4},{8,9},{9,10},{10,1... | collective-permute-start | bytes 2024 | tf_op jit(solution)/shard_map/ppermute | solution.py:20
  113.7 5.5 %collective-permute-start.34 = (f32[28,6]{1,0:T(8,128)S(1)}, f32[28,6]{1,0:T(8,128)S(1)}, u32[]{:S(2)}, u32[]{:S(2)}) collective-permute-start(f32[28,6]{1,0:T(8,128)S(1)} %get-tuple-element.1106), channel_id=1, source_target_pairs={{0,1},{1,2},{2,3},{3,0},{4,5},{5,6},{6,7},{7,4},{8,9},{9,10},{10,1... | collective-permute-start | bytes 2024 | tf_op jit(solution)/shard_map/ppermute | solution.py:20
  125.7 14.4 %collective-permute-start.38 = (f32[28,6]{1,0:T(8,128)S(1)}, f32[28,6]{1,0:T(8,128)S(1)}, u32[]{:S(2)}, u32[]{:S(2)}) collective-permute-start(f32[28,6]{1,0:T(8,128)S(1)} %get-tuple-element.1104), channel_id=1, source_target_pairs={{0,1},{1,2},{2,3},{3,0},{4,5},{5,6},{6,7},{7,4},{8,9},{9,10},{10,1... | collective-permute-start | bytes 2024 | tf_op jit(solution)/shard_map/ppermute | solution.py:20
  126.5 15.0 %collective-permute-start.39 = (f32[28,6]{1,0:T(8,128)S(1)}, f32[28,6]{1,0:T(8,128)S(1)}, u32[]{:S(2)}, u32[]{:S(2)}) collective-permute-start(f32[28,6]{1,0:T(8,128)S(1)} %get-tuple-element.1103), channel_id=1, source_target_pairs={{1,0},{2,1},{3,2},{0,3},{5,4},{6,5},{7,6},{4,7},{9,8},{10,9},{11,1... | collective-permute-start | bytes 2024 | tf_op jit(solution)/shard_map/ppermute | solution.py:23
  149.9 5.5 %collective-permute-start.42 = (f32[28,6]{1,0:T(8,128)S(1)}, f32[28,6]{1,0:T(8,128)S(1)}, u32[]{:S(2)}, u32[]{:S(2)}) collective-permute-start(f32[28,6]{1,0:T(8,128)S(1)} %get-tuple-element.1102), channel_id=1, source_target_pairs={{0,1},{1,2},{2,3},{3,0},{4,5},{5,6},{6,7},{7,4},{8,9},{9,10},{10,1... | collective-permute-start | bytes 2024 | tf_op jit(solution)/shard_map/ppermute | solution.py:20
  163.9 5.5 %collective-permute-start.46 = (f32[28,6]{1,0:T(8,128)S(1)}, f32[28,6]{1,0:T(8,128)S(1)}, u32[]{:S(2)}, u32[]{:S(2)}) collective-permute-start(f32[28,6]{1,0:T(8,128)S(1)} %get-tuple-element.1100), channel_id=1, source_target_pairs={{0,1},{1,2},{2,3},{3,0},{4,5},{5,6},{6,7},{7,4},{8,9},{9,10},{10,1... | collective-permute-start | bytes 2024 | tf_op jit(solution)/shard_map/ppermute | solution.py:20
  213.0 5.7 %collective-permute-start.58 = (f32[22,3]{1,0:T(8,128)S(1)}, f32[22,3]{1,0:T(8,128)S(1)}, u32[]{:S(2)}, u32[]{:S(2)}) collective-permute-start(f32[22,3]{1,0:T(8,128)S(1)} %get-tuple-element.1190), channel_id=1, source_target_pairs={{0,1},{1,2},{2,3},{3,0},{4,5},{5,6},{6,7},{7,4},{8,9},{9,10},{10,1... | collective-permute-start | bytes 800 | tf_op jit(solution)/shard_map/ppermute | solution.py:20
  213.8 5.7 %collective-permute-start.59 = (f32[22,3]{1,0:T(8,128)S(1)}, f32[22,3]{1,0:T(8,128)}, u32[]{:S(2)}, u32[]{:S(2)}) collective-permute-start(f32[22,3]{1,0:T(8,128)S(1)} %get-tuple-element.1189), channel_id=1, source_target_pairs={{1,0},{2,1},{3,2},{0,3},{5,4},{6,5},{7,6},{4,7},{9,8},{10,9},{11,1... | collective-permute-start | bytes 800 | tf_op jit(solution)/shard_map/ppermute | solution.py:23
  238.5 5.7 %collective-permute-start.62 = (f32[22,3]{1,0:T(8,128)S(1)}, f32[22,3]{1,0:T(8,128)S(1)}, u32[]{:S(2)}, u32[]{:S(2)}) collective-permute-start(f32[22,3]{1,0:T(8,128)S(1)} %get-tuple-element.1188), channel_id=1, source_target_pairs={{0,1},{1,2},{2,3},{3,0},{4,5},{5,6},{6,7},{7,4},{8,9},{9,10},{10,1... | collective-permute-start | bytes 800 | tf_op jit(solution)/shard_map/ppermute | solution.py:20
  263.6 5.6 %collective-permute-start.66 = (f32[22,3]{1,0:T(8,128)S(1)}, f32[22,3]{1,0:T(8,128)S(1)}, u32[]{:S(2)}, u32[]{:S(2)}) collective-permute-start(f32[22,3]{1,0:T(8,128)S(1)} %get-tuple-element.1186), channel_id=1, source_target_pairs={{0,1},{1,2},{2,3},{3,0},{4,5},{5,6},{6,7},{7,4},{8,9},{9,10},{10,1... | collective-permute-start | bytes 800 | tf_op jit(solution)/shard_map/ppermute | solution.py:20
  287.7 5.7 %collective-permute-start.70 = (f32[22,3]{1,0:T(8,128)S(1)}, f32[22,3]{1,0:T(8,128)S(1)}, u32[]{:S(2)}, u32[]{:S(2)}) collective-permute-start(f32[22,3]{1,0:T(8,128)S(1)} %get-tuple-element.1184), channel_id=1, source_target_pairs={{0,1},{1,2},{2,3},{3,0},{4,5},{5,6},{6,7},{7,4},{8,9},{9,10},{10,1... | collective-permute-start | bytes 800 | tf_op jit(solution)/shard_map/ppermute | solution.py:20
  288.4 5.7 %collective-permute-start.71 = (f32[22,3]{1,0:T(8,128)S(1)}, f32[22,3]{1,0:T(8,128)}, u32[]{:S(2)}, u32[]{:S(2)}) collective-permute-start(f32[22,3]{1,0:T(8,128)S(1)} %get-tuple-element.1183), channel_id=1, source_target_pairs={{1,0},{2,1},{3,2},{0,3},{5,4},{6,5},{7,6},{4,7},{9,8},{10,9},{11,1... | collective-permute-start | bytes 800 | tf_op jit(solution)/shard_map/ppermute | solution.py:23
  311.1 5.7 %collective-permute-start.74 = (f32[22,3]{1,0:T(8,128)S(1)}, f32[22,3]{1,0:T(8,128)S(1)}, u32[]{:S(2)}, u32[]{:S(2)}) collective-permute-start(f32[22,3]{1,0:T(8,128)S(1)} %get-tuple-element.1182), channel_id=1, source_target_pairs={{0,1},{1,2},{2,3},{3,0},{4,5},{5,6},{6,7},{7,4},{8,9},{9,10},{10,1... | collective-permute-start | bytes 800 | tf_op jit(solution)/shard_map/ppermute | solution.py:20
  331.6 5.6 %collective-permute-start.78 = (f32[22,3]{1,0:T(8,128)S(1)}, f32[22,3]{1,0:T(8,128)S(1)}, u32[]{:S(2)}, u32[]{:S(2)}) collective-permute-start(f32[22,3]{1,0:T(8,128)S(1)} %get-tuple-element.1180), channel_id=1, source_target_pairs={{0,1},{1,2},{2,3},{3,0},{4,5},{5,6},{6,7},{7,4},{8,9},{9,10},{10,1... | collective-permute-start | bytes 800 | tf_op jit(solution)/shard_map/ppermute | solution.py:20
  352.0 5.6 %collective-permute-start.82 = (f32[22,3]{1,0:T(8,128)S(1)}, f32[22,3]{1,0:T(8,128)S(1)}, u32[]{:S(2)}, u32[]{:S(2)}) collective-permute-start(f32[22,3]{1,0:T(8,128)S(1)} %get-tuple-element.1178), channel_id=1, source_target_pairs={{0,1},{1,2},{2,3},{3,0},{4,5},{5,6},{6,7},{7,4},{8,9},{9,10},{10,1... | collective-permute-start | bytes 800 | tf_op jit(solution)/shard_map/ppermute | solution.py:20
  374.0 5.6 %collective-permute-start.86 = (f32[22,3]{1,0:T(8,128)S(1)}, f32[22,3]{1,0:T(8,128)S(1)}, u32[]{:S(2)}, u32[]{:S(2)}) collective-permute-start(f32[22,3]{1,0:T(8,128)S(1)} %get-tuple-element.1176), channel_id=1, source_target_pairs={{0,1},{1,2},{2,3},{3,0},{4,5},{5,6},{6,7},{7,4},{8,9},{9,10},{10,1... | collective-permute-start | bytes 800 | tf_op jit(solution)/shard_map/ppermute | solution.py:20
  396.0 5.6 %collective-permute-start.90 = (f32[22,3]{1,0:T(8,128)S(1)}, f32[22,3]{1,0:T(8,128)S(1)}, u32[]{:S(2)}, u32[]{:S(2)}) collective-permute-start(f32[22,3]{1,0:T(8,128)S(1)} %get-tuple-element.1174), channel_id=1, source_target_pairs={{0,1},{1,2},{2,3},{3,0},{4,5},{5,6},{6,7},{7,4},{8,9},{9,10},{10,1... | collective-permute-start | bytes 800 | tf_op jit(solution)/shard_map/ppermute | solution.py:20
  419.1 5.6 %collective-permute-start.94 = (f32[22,3]{1,0:T(8,128)S(1)}, f32[22,3]{1,0:T(8,128)S(1)}, u32[]{:S(2)}, u32[]{:S(2)}) collective-permute-start(f32[22,3]{1,0:T(8,128)S(1)} %get-tuple-element.1172), channel_id=1, source_target_pairs={{0,1},{1,2},{2,3},{3,0},{4,5},{5,6},{6,7},{7,4},{8,9},{9,10},{10,1... | collective-permute-start | bytes 800 | tf_op jit(solution)/shard_map/ppermute | solution.py:20
  (154 other events, 620.4 us)
where the time goes:
time: 447 us; the launch traced here: 438 us
  starting transfers between devices  175 us (39%)
  other arithmetic  166 us (37%)
  waiting for transfers between devices  58.8 us (13%)
  local copies, waits for them, and re-layouts  34.9 us (8%)
    ppermute x48, starting transfers between devices, extended(): lax.ppermute(lax.slice_in_dim(block, 0, width, axis=dim), axis, backward)  152 us
    ppermute x48, waiting for transfers between devices, extended(): lax.ppermute(lax.slice_in_dim(block, block.shape[dim] - width, None, axis...  54.6 us
    add_any x24, other arithmetic, weno(): cand_three = third / 3.0 + 5.0 * fourth / 6.0 - fifth / 6.0  52 us
    add_any x96, other arithmetic, weno(): cand_one = first / 3.0 - 7.0 * second / 6.0 + 11.0 * third / 6.0  34.2 us
    ppermute x48, starting transfers between devices, extended(): lax.ppermute(lax.slice_in_dim(block, block.shape[dim] - width, None, axis...  23.5 us
    add_any x48, other arithmetic, weno(): cand_two = -second / 6.0 + 5.0 * third / 6.0 + fourth / 3.0  19.4 us
    concatenate x24, local copies, waits for them, and re-layouts, extended(): block = jnp.concatenate([low, block, high], axis=dim)  16.3 us
    unnamed x180, local copies, waits for them, and re-layouts  15.6 us
  transfers between devices with their start and end apart: 96, of which 50 were waited for; matrix products, arithmetic and copies ran while one was open for 5% of the time, Pallas kernels for 0%

commit v1 on v0

v1 whole, which is shorter than its diff:
```python
import functools

import jax
import jax.numpy as jnp
from jax import lax
from jax.experimental import pallas as pl
from jax.experimental.pallas import tpu as pltpu
from jax.sharding import PartitionSpec as P

STEPS = 6
STAGES = 2 * STEPS
time_step = 0.2
smooth_eps = 0.001
speed_floor = 0.25
LANES = 128
SHIFTS = (-3, -2, -1, 1, 2, 3)


def blend(m, q1, q2, q3, t1, t2, t3):
    t23 = t2 * t3
    inverse = 1.0 / (t1 * t23)
    r1 = t23 * inverse
    r2 = (t1 * t3) * inverse
    r3 = (t1 * t2) * inverse
    a1 = 0.1 * (r1 * r1)
    a2 = 0.6 * (r2 * r2)
    a3 = 0.3 * (r3 * r3)
    total = 1.0 / (a1 + a2 + a3)
    w1, w2, w3 = a1 * total, a2 * total, a3 * total
    offset = w1 * q1 + w2 * q2 + w3 * q3
    return m + offset, (offset, w1, w2, w3, r1, r2, r3, q1, q2, q3)


def values(u):
    m = [u[k + 1] - u[k] for k in range(6)]
    e = [m[k + 1] - m[k] for k in range(5)]
    sq = [x * x for x in e]
    low = [(4.0 / 3.0) * x + smooth_eps for x in sq]
    high = [(10.0 / 3.0) * x for x in sq]
    prod = [e[k] * e[k + 1] for k in range(4)]
    far = [(11.0 / 3.0) * x for x in prod]
    t1 = low[0] + high[1] - far[0]
    t2 = low[1] + (low[2] - smooth_eps) - (5.0 / 3.0) * prod[1]
    t3 = low[3] + high[2] - far[2]
    s1 = low[4] + high[3] - far[3]
    s2 = low[2] + (low[3] - smooth_eps) - (5.0 / 3.0) * prod[2]
    s3 = low[1] + high[2] - far[1]
    third = [x * (1.0 / 3.0) for x in e]
    sixth = [x * (1.0 / 6.0) for x in e]
    left, keep_left = blend(
        m[2],
        (5.0 / 6.0) * e[1] - third[0],
        sixth[1] + third[2],
        (2.0 / 3.0) * e[2] - sixth[3],
        t1, t2, t3,
    )
    right, keep_right = blend(
        -m[3],
        (5.0 / 6.0) * e[3] - third[4],
        sixth[3] + third[2],
        (2.0 / 3.0) * e[2] - sixth[1],
        s1, s2, s3,
    )
    return jnp.maximum(left, 0.0), jnp.maximum(right, 0.0), e, keep_left, keep_right


def side_grads(factor, keep, e0, e1, e2, e3):
    offset, w1, w2, w3, r1, r2, r3, q1, q2, q3 = keep
    w1, w2, w3 = factor * w1, factor * w2, factor * w3
    k1 = (-2.0 * w1) * ((q1 - offset) * r1)
    k2 = (-2.0 * w2) * ((q2 - offset) * r2)
    k3 = (-2.0 * w3) * ((q3 - offset) * r3)
    g0 = k1 * ((8.0 / 3.0) * e0 - (11.0 / 3.0) * e1) - w1 * (1.0 / 3.0)
    g1 = (
        k1 * ((20.0 / 3.0) * e1 - (11.0 / 3.0) * e0)
        + k2 * ((8.0 / 3.0) * e1 - (5.0 / 3.0) * e2)
        + ((5.0 / 6.0) * w1 + (1.0 / 6.0) * w2)
    )
    g2 = (
        k2 * ((8.0 / 3.0) * e2 - (5.0 / 3.0) * e1)
        + k3 * ((20.0 / 3.0) * e2 - (11.0 / 3.0) * e3)
        + ((1.0 / 3.0) * w2 + (2.0 / 3.0) * w3)
    )
    g3 = k3 * ((8.0 / 3.0) * e3 - (11.0 / 3.0) * e2) - w3 * (1.0 / 6.0)
    return g0, g1, g2, g3


def cell_grads(part, inverse):
    left, right, e, keep_left, keep_right = part
    p, n = left * inverse, right * inverse
    a0, a1, a2, a3 = side_grads(p, keep_left, e[0], e[1], e[2], e[3])
    b0, b1, b2, b3 = side_grads(n, keep_right, e[4], e[3], e[2], e[1])
    ge = (a0, a1 + b3, a2 + b2, a3 + b1, b0)
    gm = (-ge[0], ge[0] - ge[1], ge[1] - ge[2] + p, ge[2] - ge[3] - n, ge[3] - ge[4], ge[4])
    return (-gm[0],) + tuple(gm[k] - gm[k + 1] for k in range(5)) + (gm[5],)


def kernel(
    sizes, level_ref, rate_ref, cot_ref, final_ref, rgrad_ref, igrad_ref,
    pad, coef, value, edge_out, edge_in, adj, mid, wgt, acc,
    row_out, row_in, col_out, col_in, send_sem, recv_sem,
):
    count_y, count_x = sizes
    rows, subs = level_ref.shape[0], level_ref.shape[1]
    own = pl.ds(8, subs)
    iy, ix = lax.axis_index("gy"), lax.axis_index("gx")
    prev_y = {"gy": lax.rem(iy + count_y - 1, count_y)}
    next_y = {"gy": lax.rem(iy + 1, count_y)}
    prev_x = {"gx": lax.rem(ix + count_x - 1, count_x)}
    next_x = {"gx": lax.rem(ix + 1, count_x)}
    targets = (prev_y, next_y, prev_x, next_x)

    barrier = pltpu.get_barrier_semaphore()
    for target in targets:
        pl.semaphore_signal(barrier, inc=1, device_id=target, device_id_type=pl.DeviceIdType.MESH)
    pl.semaphore_wait(barrier, 4)

    lane = lax.broadcasted_iota(jnp.int32, (subs, LANES), 1)
    sub = lax.broadcasted_iota(jnp.int32, (subs, LANES), 0)

    def copies(pairs, slot):
        return [
            pltpu.make_async_remote_copy(
                src_ref=source,
                dst_ref=target,
                send_sem=send_sem.at[slot, way],
                recv_sem=recv_sem.at[slot, way],
                device_id=targets[way],
                device_id_type=pl.DeviceIdType.MESH,
            )
            for way, (source, target) in enumerate(pairs)
        ]

    def state_copies(t, slot):
        return copies(
            (
                (pad.at[t, pl.ds(3, 3)], pad.at[t, pl.ds(3 + rows, 3)]),
                (pad.at[t, pl.ds(rows, 3)], pad.at[t, pl.ds(0, 3)]),
                (edge_out.at[t, 0], edge_in.at[t, 1]),
                (edge_out.at[t, 1], edge_in.at[t, 0]),
            ),
            slot,
        )

    def put(t, r, new):
        pad[t, 3 + r, own] = new
        edge_out[t, 0, pl.ds(r, 1)] = new[0:1]
        edge_out[t, 1, pl.ds(r, 1)] = new[subs - 1 : subs]

    def column_shift(here, before, after, k):
        if k < 0:
            return pltpu.roll(jnp.where(lane >= LANES + k, before, here), -k, 1)
        return pltpu.roll(jnp.where(lane < k, after, here), LANES - k, 1)

    def stage(t, slot, advance):
        moves = state_copies(t, slot)
        for move in moves:
            move.start()
        for move in moves:
            move.wait()
        pad[t, pl.ds(3, rows), 7] = edge_in[t, 0]
        pad[t, pl.ds(3, rows), 8 + subs] = edge_in[t, 1]

        def row(r, carry):
            here = pad[t, 3 + r, own]
            before = pad[t, 3 + r, pl.ds(7, subs)]
            after = pad[t, 3 + r, pl.ds(9, subs)]
            part_y = values([here if k == 3 else pad[t, r + k, own] for k in range(7)])
            part_x = values(
                [here if k == 0 else column_shift(here, before, after, k) for k in range(-3, 4)]
            )
            square = part_y[0] * part_y[0] + part_y[1] * part_y[1]
            square = square + part_x[0] * part_x[0] + part_x[1] * part_x[1]
            speed = jnp.sqrt(square + speed_floor)
            value[t, r] = speed
            advance(r, here, speed)
            inverse = 1.0 / speed
            grad_y = cell_grads(part_y, inverse)
            grad_x = cell_grads(part_x, inverse)
            for i, k in enumerate(SHIFTS):
                coef[t, i, r] = grad_y[k + 3]
                coef[t, 6 + i, r] = grad_x[k + 3]
            coef[t, 12, r] = grad_y[3] + grad_x[3]
            return carry

        lax.fori_loop(0, rows, row, 0)

    def first_row(r, carry):
        put(0, r, level_ref[r])
        return carry

    lax.fori_loop(0, rows, first_row, 0)

    def forward(step, carry):
        t = 2 * step

        def early(r, here, speed):
            put(t + 1, r, here - time_step * rate_ref[r] * speed)

        def late(r, here, speed):
            new = 0.5 * pad[t, 3 + r, own] + 0.5 * (here - time_step * rate_ref[r] * speed)
            put(t + 2, r, new)

        stage(t, 0, early)
        stage(t + 1, 1, late)
        return carry

    lax.fori_loop(0, STEPS, forward, 0)

    def pull_back(t, slot):
        def column(i):
            total = None
            for j, k in enumerate(SHIFTS):
                if 0 <= i - k < rows:
                    term = coef[t, j, i - k] * wgt[i - k]
                    total = term if total is None else total + term
            return total

        for k in range(3):
            row_out[t, 0, k] = column(k - 3)
            row_out[t, 1, k] = column(rows + k)
        moves = copies(
            (
                (row_out.at[t, 0], row_in.at[t, 1]),
                (row_out.at[t, 1], row_in.at[t, 0]),
                (col_out.at[t, 0], col_in.at[t, 1]),
                (col_out.at[t, 1], col_in.at[t, 0]),
            ),
            slot,
        )
        moves[0].start()
        moves[1].start()

        def row(r, carry):
            weight = wgt[r]
            total = coef[t, 12, r] * weight
            over = under = None
            for j, k in enumerate(SHIFTS):
                moved = pltpu.roll(coef[t, 6 + j, r] * weight, k % LANES, 1)
                outside = lane < k if k > 0 else lane >= LANES + k
                leaving = jnp.where(outside, moved, 0.0)
                total = total + jnp.where(outside, 0.0, moved)
                if k > 0:
                    over = leaving if over is None else over + leaving
                else:
                    under = leaving if under is None else under + leaving
            total = total + jnp.where(sub == 0, 0.0, pltpu.roll(over, 1, 0))
            total = total + jnp.where(sub == subs - 1, 0.0, pltpu.roll(under, subs - 1, 0))
            acc[r] = total
            col_out[t, 0, pl.ds(r, 1)] = under[0:1]
            col_out[t, 1, pl.ds(r, 1)] = over[subs - 1 : subs]
            return carry

        lax.fori_loop(0, rows, row, 0, unroll=2)
        moves[2].start()
        moves[3].start()
        for i in range(rows):
            acc[i] += column(i)
        for move in moves:
            move.wait()
        for k in range(3):
            acc[k] += row_in[t, 0, k]
            acc[rows - 3 + k] += row_in[t, 1, k]
        acc[:, 0] += col_in[t, 0]
        acc[:, subs - 1] += col_in[t, 1]

    def start_row(r, carry):
        final_ref[r] = pad[STAGES, 3 + r, own]
        adj[r] = cot_ref[r]
        rgrad_ref[r] = jnp.zeros((subs, LANES), jnp.float32)
        weight = (0.5 * time_step) * cot_ref[r]
        wgt[r] = rate_ref[r] * weight
        return carry

    lax.fori_loop(0, rows, start_row, 0)

    def backward(index, carry):
        t = 2 * (STEPS - 1 - index)
        pull_back(t + 1, 0)

        def late_row(r, inner):
            weight_late = (0.5 * time_step) * adj[r]
            middle = 0.5 * adj[r] - acc[r]
            weight = time_step * middle
            rgrad_ref[r] = rgrad_ref[r] - weight_late * value[t + 1, r] - weight * value[t, r]
            mid[r] = middle
            wgt[r] = rate_ref[r] * weight
            return inner

        lax.fori_loop(0, rows, late_row, 0, unroll=2)
        pull_back(t, 1)

        def early_row(r, inner):
            new = 0.5 * adj[r] + mid[r] - acc[r]
            adj[r] = new
            wgt[r] = rate_ref[r] * ((0.5 * time_step) * new)
            return inner

        lax.fori_loop(0, rows, early_row, 0, unroll=2)
        return carry

    lax.fori_loop(0, STEPS, backward, 0)

    def end_row(r, carry):
        igrad_ref[r] = adj[r]
        return carry

    lax.fori_loop(0, rows, end_row, 0)


def solution(mesh):
    sizes = (mesh.shape["gy"], mesh.shape["gx"])

    def shards(level_set, spread_rate, cotangent):
        rows, columns = level_set.shape
        subs = columns // LANES
        block = (rows, subs, LANES)
        f32 = jnp.float32
        outs = pl.pallas_call(
            functools.partial(kernel, sizes),
            out_shape=[jax.ShapeDtypeStruct(block, f32)] * 3,
            in_specs=[pl.BlockSpec(memory_space=pltpu.VMEM)] * 3,
            out_specs=[pl.BlockSpec(memory_space=pltpu.VMEM)] * 3,
            scratch_shapes=[
                pltpu.VMEM((STAGES + 1, rows + 6, subs + 16, LANES), f32),
                pltpu.VMEM((STAGES, 13) + block, f32),
                pltpu.VMEM((STAGES,) + block, f32),
                pltpu.VMEM((STAGES + 1, 2, rows, LANES), f32),
                pltpu.VMEM((STAGES, 2, rows, LANES), f32),
                pltpu.VMEM(block, f32),
                pltpu.VMEM(block, f32),
                pltpu.VMEM(block, f32),
                pltpu.VMEM(block, f32),
                pltpu.VMEM((STAGES, 2, 3, subs, LANES), f32),
                pltpu.VMEM((STAGES, 2, 3, subs, LANES), f32),
                pltpu.VMEM((STAGES, 2, rows, LANES), f32),
                pltpu.VMEM((STAGES, 2, rows, LANES), f32),
                pltpu.SemaphoreType.DMA((2, 4)),
                pltpu.SemaphoreType.DMA((2, 4)),
            ],
            compiler_params=pltpu.CompilerParams(
                collective_id=0, has_side_effects=True, vmem_limit_bytes=60 * 2**20
            ),
        )(*(x.reshape(block) for x in (level_set, spread_rate, cotangent)))
        return tuple(x.reshape(rows, columns) for x in outs)

    spec = P("gy", "gx")
    return jax.shard_map(
        shards, mesh=mesh, in_specs=(spec,) * 3, out_specs=(spec,) * 3, check_vma=False
    )
```

time: 447 us -> 149 us (0.33); the launches traced: 438 us -> 149 us
  starting transfers between devices: 175 us -> 0 us
  other arithmetic: 166 us -> 0 us
  Pallas kernels: 0 us -> 143 us
  waiting for transfers between devices: 58.8 us -> 0 us
  local copies, waits for them, and re-layouts: 34.9 us -> 5.69 us
    ppermute x96 -> x0, starting transfers between devices: 175 us -> none  [the longest x48 152 us: extended(): lax.ppermute(lax.slice_in_dim(block, 0, width, axis=dim), axis, backward)]
    pallas_call x0 -> x1, Pallas kernels: none -> 143 us  [shards(): pl.pallas_call(functools.partial(kernel, sizes), out_shape=[jax.ShapeDtyp...]
    add_any x192 -> x0, other arithmetic: 108 us -> none  [the longest x24 52 us: weno(): cand_three = third / 3.0 + 5.0 * fourth / 6.0 - fifth / 6.0]
    ppermute x96 -> x0, waiting for transfers between devices: 58.8 us -> none  [the longest x48 54.6 us: extended(): lax.ppermute(lax.slice_in_dim(block, block.shape[dim] - width, None, axis...]
    add x17 -> x0, other arithmetic: 21.8 us -> none  [the longest x12 14.6 us: weno(): alpha_one + alpha_two + alpha_three]
    sub x56 -> x0, other arithmetic: 18.6 us -> none  [the longest x6 7.8 us: shards(): middle = state - time_step * spread_rate * speed(padded)]
    concatenate x24 -> x0, local copies, waits for them, and re-layouts: 16.3 us -> none  [extended(): block = jnp.concatenate([low, block, high], axis=dim)]
    unnamed x180 -> x12, local copies, waits for them, and re-layouts: 15.6 us -> 4.91 us
  transfers between devices with their start and end apart: 96 -> 0, of which waited for: 50 -> 0; matrix products, arithmetic and copies ran while one was open for 5% -> 0% of each run, Pallas kernels for 0% -> 0%
where the time goes in v1:
time: 149 us
  Pallas kernels  143 us (96%)
  local copies, waits for them, and re-layouts  5.69 us (4%)
    pallas_call x1, Pallas kernels, shards(): pl.pallas_call(functools.partial(kernel, sizes), out_shape=[jax.ShapeDtyp...  143 us
    unnamed x12, local copies, waits for them, and re-layouts  4.91 us

profile of v1, /device:TPU:0, one launch (start us, length us, event | category | flops | bytes accessed | tf_op | source)
XLA Modules:
  0.0 148.9 jit_solution(16457853679279185925)
XLA Ops:
  0.6 0.0 copy-start
  0.6 1.6 %copy.6 = f32[2,8,16,128]{3,2,1,0:T(8,128)} copy(f32[2,8,16,128]{3,1,2,0:T(8,128)} %bitcast.19) | data formatting | bytes 262144
  2.3 0.0 copy-done
  2.3 0.0 copy-start.1
  2.3 0.7 copy.7
  2.9 0.3 copy-done.1
  3.2 0.7 copy.8
  3.9 142.6 %shard_map.58 = (f32[16,16,128]{2,1,0:T(8,128)}, f32[16,16,128]{2,1,0:T(8,128)}, f32[16,16,128]{2,1,0:T(8,128)}) custom-call(f32[16,16,128]{2,1,0:T(8,128)} %bitcast.16, f32[16,16,128]{2,1,0:T(8,128)} %bitcast.17, f32[16,16,128]{2,1,0:T(8,128)} %bitcast.18), custom_call_target="tpu_custom_call" | custom-call | tf_op jit(solution)/shard_map/pallas_call | solution.py:319
  146.5 0.0 copy-start.2
  146.5 0.0 copy-start.3
  146.5 1.6 %copy.15 = f32[2,8,16,128]{3,1,2,0:T(8,128)} copy(f32[2,8,16,128]{3,2,1,0:T(8,128)} %bitcast.23) | data formatting | bytes 262144
  148.1 0.0 copy-done.2
  148.1 0.0 copy-done.3
  148.1 0.8 copy_bitcast_fusion
Async XLA Ops:
  0.6 1.6 %copy-start = (f32[16,2048]{1,0:T(8,128)S(1)}, f32[16,2048]{1,0:T(8,128)}, u32[]{:S(2)}) copy-start(f32[16,2048]{1,0:T(8,128)} %param.4) | copy-start | bytes 393220
  2.3 1.0 copy-start.1
  146.5 1.7 %copy-start.2 = (f32[16,16,128]{2,1,0:T(8,128)S(1)}, f32[16,16,128]{2,1,0:T(8,128)}, u32[]{:S(2)}) copy-start(f32[16,16,128]{2,1,0:T(8,128)} %get-tuple-element.7) | copy-start | bytes 393220
  146.5 1.7 %copy-start.3 = (f32[16,16,128]{2,1,0:T(8,128)S(1)}, f32[16,16,128]{2,1,0:T(8,128)}, u32[]{:S(2)}) copy-start(f32[16,16,128]{2,1,0:T(8,128)} %get-tuple-element.8) | copy-start | bytes 393220
